TPU v7x, 32 devices: a whole 2x2x4 slice. The times are simulated.
32 devices in a mesh: groups: 2 (over y), ctx: 16 (over z, x, core).
Axes of the slice: x: 2, y: 2, z: 4, core: 2. Of those that a mesh axis runs over, the one named last changes fastest.
Arguments:
- queries: bfloat16 [32, 8192], P(('groups', 'ctx')), parts along dimension 0, may hold values from -120 to 120
- fresh_keys: bfloat16 [32, 512], P(('groups', 'ctx')), parts along dimension 0, may hold values from -4 to 4
- fresh_values: bfloat16 [32, 512], P(('groups', 'ctx')), parts along dimension 0, may hold values from -4 to 4
- cache_keys: bfloat16 [32768, 512], P(('groups', 'ctx')), parts along dimension 0, may hold values from -4 to 4
- stored_values: bfloat16 [32768, 512], P(('groups', 'ctx')), parts along dimension 0, may hold values from -4 to 4
- cache_lengths: int32 [32], P(('groups', 'ctx')), parts along dimension 0, may hold values from 1 to 1024, as said below
- positions: int32 [32], P('groups'), parts along dimension 0, may hold values from 0 to 15, each once
Outputs:
- attended: bfloat16 [32, 8192], P(('groups', 'ctx')), parts along dimension 0
There are 2 independent parts, one for each index of `groups`. A program takes and returns all parts, laid end to end along the dimension named above; each array names one. Nothing has to cross between parts.
Inputs may be any that keep to these rules, and one draw needn't show every extreme that they name: `cache_lengths`: each entry lies between 1 and 1024, and one shard has all 1024 slots live.
All inputs are finite; a program needn't handle non-finite values.
Results may differ from a plain program's by a relative error of at most 0.003.
Values may be sent and summed in bfloat16 or wider, within the bound.
A program may use at most 128 MiB of HBM per device.

v0:
```python
import jax
import jax.numpy as jnp
from jax import lax
from jax.sharding import PartitionSpec as P

HEADS_PER_GROUP = 16
HEAD_WIDTH = 128


def body(queries, fresh_keys, fresh_values, cache_keys, stored_values, cache_lengths, positions):
    device_rank = lax.axis_index("ctx")
    new_rows = fresh_keys.shape[0]
    cache_rows = cache_keys.shape[0]
    head_size = HEAD_WIDTH
    group_size = HEADS_PER_GROUP
    kv_heads = fresh_keys.shape[1] // head_size
    query_heads = kv_heads * group_size
    all_keys = jnp.concatenate([cache_keys, fresh_keys], axis=0)
    all_values = jnp.concatenate([stored_values, fresh_values], axis=0)
    gathered = lax.all_gather(queries, "ctx", axis=0, tiled=True)
    total_new = gathered.shape[0]
    key_order = lax.dynamic_slice_in_dim(positions, device_rank * new_rows, new_rows, 0)
    live = jnp.arange(cache_rows, dtype=jnp.int32) < cache_lengths[0]
    cache_seen = jnp.broadcast_to(live[None, :], (total_new, cache_rows))
    new_seen = key_order[None, :] <= positions[:, None]
    visible = jnp.concatenate([cache_seen, new_seen], axis=1)
    maxima_list = []
    totals_list = []
    sums_list = []
    for head_group in range(kv_heads):
        query_part = gathered[
            :, head_group * group_size * head_size : (head_group + 1) * group_size * head_size
        ].reshape(total_new, group_size, head_size)
        key_part = all_keys[:, head_group * head_size : (head_group + 1) * head_size]
        value_part = all_values[:, head_group * head_size : (head_group + 1) * head_size]
        scores = jnp.einsum(
            "ngd,kd->ngk", query_part, key_part, preferred_element_type=jnp.float32
        ) * head_size ** (-0.5)
        scores = jnp.where(visible[:, None, :], scores, -jnp.inf)
        maxima = jnp.max(scores, axis=-1)
        weights = jnp.exp(scores - maxima[..., None]).astype(jnp.bfloat16)
        totals = jnp.sum(weights.astype(jnp.float32), axis=-1)
        sums = jnp.einsum("ngk,kd->ngd", weights, value_part, preferred_element_type=jnp.float32)
        maxima_list.append(maxima)
        totals_list.append(totals)
        sums_list.append(sums.reshape(total_new, group_size * head_size))
    block_max = jnp.concatenate(maxima_list, axis=1)
    block_total = jnp.concatenate(totals_list, axis=1)
    block_sum = jnp.concatenate(sums_list, axis=1)
    sums_in, maxima_in, totals_in = (
        lax.all_to_all(block_sum[None], "ctx", split_axis=1, concat_axis=0, tiled=True),
        lax.all_to_all(block_max[None], "ctx", split_axis=1, concat_axis=0, tiled=True),
        lax.all_to_all(block_total[None], "ctx", split_axis=1, concat_axis=0, tiled=True),
    )
    overall = jnp.max(maxima_in, axis=0)
    scale = jnp.exp(maxima_in - overall[None])
    sources = sums_in.shape[0]
    numerator = jnp.sum(
        sums_in.reshape(sources, new_rows, query_heads, head_size) * scale[..., None], axis=0
    )
    denominator = jnp.sum(totals_in * scale, axis=0)
    result = numerator / denominator[..., None]
    return result.reshape(new_rows, query_heads * head_size).astype(jnp.bfloat16)


def solution(mesh):
    return jax.shard_map(
        body,
        mesh=mesh,
        in_specs=(
            P(("groups", "ctx"), None),
            P(("groups", "ctx"), None),
            P(("groups", "ctx"), None),
            P(("groups", "ctx"), None),
            P(("groups", "ctx"), None),
            P(("groups", "ctx")),
            P("groups"),
        ),
        out_specs=P(("groups", "ctx"), None),
        check_vma=False,
    )
```

profile of v0, /device:TPU:0, one launch (start us, length us, event | category | flops | bytes accessed | tf_op | source)
XLA Modules:
  0.0 74.4 jit_solution(8473984056943046898)
XLA Ops:
  0.7 1.2 %dynamic_slice.3 = s32[1]{0:T(128)} dynamic-slice(s32[16]{0:T(128)} %param.13, s32[]{:T(128)S(6)} %select_n.16), dynamic_slice_sizes={1} | dynamic-slice | bytes 12 | tf_op jit(solution)/shard_map/dynamic_slice | solution.py:22
  1.9 1.3 %compare_bitcast_fusion = pred[16,1]{0,1:T(4,128)(4,1)S(1)} fusion(s32[16]{0:T(128)} %param.13, s32[]{:T(128)} %bitcast.1), kind=kLoop, calls=%fused_computation.57 | loop fusion | flops 16 | bytes 84 | tf_op jit(solution)/shard_map/le | solution.py:25
  3.2 0.1 copy.10
  3.3 24.9 %all-gather = bf16[16,1,8192]{2,1,0:T(2,128)(2,1)S(1)} all-gather(bf16[1,1,8192]{2,1,0:T(2,128)(2,1)} %bitcast.115), channel_id=1, replica_groups=mesh['groups'=2,'ctx'=16] {'ctx'}, dimensions={0}, use_global_device_ids=true | all-gather | bytes 278528 | tf_op jit(solution)/shard_map/all_gather | solution.py:20
  28.2 0.3 copy.25
  28.6 0.0 copy-start.6
  28.7 0.0 copy-done.1
  28.7 0.1 constant_dynamic-update-slice_fusion.1
  28.8 0.5 copy-done.6
  29.3 0.4 fusion.15
  29.7 0.4 fusion.16
  30.2 0.0 copy-start.2
  30.2 0.4 fusion.17
  30.6 1.4 %fusion.18 = (f32[16,16]{1,0:T(8,128)S(1)}, f32[16,16,1025]{2,1,0:T(8,128)}) fusion(bf16[16,16,128]{2,1,0:T(8,128)(2,1)S(1)} %bitcast.105, bf16[1025,512]{1,0:T(8,128)(2,1)S(1)} %constant_dynamic-update-slice_fusion, pred[16,1025]{1,0:T(8,128)(4,1)S(1)} %pad_add_fusion), kind=kOutput, calls=%fused_computation.61 | convolution fusion | flops 67961344 | bytes 1398784 | tf_op jit(solution)/shard_map/ngd,kd->ngk/dot_general | solution.py:36
  32.0 0.0 copy-done.2
  32.0 0.7 pad_maximum_fusion.1
  32.6 0.0 copy-done.4
  32.6 4.1 %all-to-all-start.1 = ((f32[1,16,64]{2,0,1:T(1,128)}), f32[1,16,64]{2,0,1:T(1,128)}, u32[]{:S(2)}, u32[]{:S(2)}) async-start(f32[1,16,64]{2,0,1:T(1,128)} %bitcast.116), calls=%async_computation.1 | async-start | bytes 16384 | tf_op jit(solution)/shard_map/all_to_all | solution.py:52
  36.7 0.0 copy-start.7
  36.7 1.3 %constant_dynamic-update-slice_fusion.3 = bf16[1025,512]{1,0:T(8,128)(2,1)S(1)} fusion(bf16[1024,512]{1,0:T(8,128)(2,1)} %param.11), kind=kLoop, calls=%fused_computation.48 | loop fusion | bytes 2097152
  38.0 0.0 copy-done.7
  38.1 0.0 copy-start.3
  38.1 0.4 fusion.8
  38.5 0.3 copy-done.3
  38.8 0.5 convert_reduce_fusion
  39.2 0.0 copy-start
  39.2 0.0 copy-start.5
  39.2 0.4 fusion.9
  39.6 0.9 %copy-done = f32[16,16,1025]{2,1,0:T(8,128)S(1)} copy-done((f32[16,16,1025]{2,1,0:T(8,128)S(1)}, f32[16,16,1025]{2,1,0:T(8,128)}, u32[]{:S(2)}) %copy-start) | copy-done | bytes 1049624
  40.5 0.4 fusion.11
  40.9 0.5 convert_reduce_fusion.2
  41.4 0.4 fusion.10
  41.7 0.1 copy_bitcast_fusion.1
  41.8 0.1 copy_bitcast_fusion.3
  41.9 0.7 pad_maximum_fusion.2
  42.6 0.6 all-to-all-done.1
  43.2 5.4 %all-to-all-start.2 = ((f32[1,16,64]{2,0,1:T(1,128)}), f32[1,16,64]{2,0,1:T(1,128)S(1)}, u32[]{:S(2)}, u32[]{:S(2)}) async-start(f32[1,16,64]{2,0,1:T(1,128)} %bitcast.20), calls=%async_computation.2 | async-start | bytes 16384 | tf_op jit(solution)/shard_map/all_to_all | solution.py:53
  48.6 1.3 %broadcast_in_dim.55 = f32[1,16,8192]{2,0,1:T(1,128)} reshape(f32[16,8192]{1,0:T(8,128)S(1)} %pad_maximum_fusion) | data formatting | bytes 1048576 | tf_op jit(solution)/shard_map/broadcast_in_dim | solution.py:51
  49.9 5.0 %all-to-all-done.2 = f32[1,16,64]{2,0,1:T(1,128)S(1)} async-done(((f32[1,16,64]{2,0,1:T(1,128)}), f32[1,16,64]{2,0,1:T(1,128)S(1)}, u32[]{:S(2)}, u32[]{:S(2)}) %all-to-all-start.2) | async-done | bytes 4128 | tf_op jit(solution)/shard_map/all_to_all | solution.py:53
  54.9 3.6 %all-to-all-start = ((f32[1,16,8192]{2,0,1:T(1,128)}), f32[1,16,8192]{2,0,1:T(1,128)S(1)}, u32[]{:S(2)}, u32[]{:S(2)}) async-start(f32[1,16,8192]{2,0,1:T(1,128)} %broadcast_in_dim.55), calls=%async_computation | async-start | bytes 1048576 | tf_op jit(solution)/shard_map/all_to_all | solution.py:51
  58.5 0.7 reduce_max.49
  59.2 0.7 fusion.14
  59.9 0.7 subtract_exponential_fusion
  60.6 12.1 %all-to-all-done = f32[1,16,8192]{2,0,1:T(1,128)S(1)} async-done(((f32[1,16,8192]{2,0,1:T(1,128)}), f32[1,16,8192]{2,0,1:T(1,128)S(1)}, u32[]{:S(2)}, u32[]{:S(2)}) %all-to-all-start) | async-done | bytes 524320 | tf_op jit(solution)/shard_map/all_to_all | solution.py:51
  72.7 0.2 mul.59
  72.9 0.8 %multiply_reduce_fusion = f32[8192]{0:T(1024)S(1)} fusion(f32[1,16,8192]{2,0,1:T(1,128)S(1)} %all-to-all-done, f32[1,16,8192]{2,0,1:T(1,128)S(1)} %bitcast.103), kind=kLoop, calls=%fused_computation.21 | loop fusion | flops 253952 | bytes 1081344 | tf_op jit(solution)/shard_map/reduce_sum | solution.py:58
  73.7 0.1 div.20
  73.7 0.7 divide_convert_fusion
  (14 shorter events, 0.2 us)
Async XLA Ops:
  3.3 25.4 %copy-start.1 = (bf16[1024,512]{1,0:T(8,128)(2,1)S(1)}, bf16[1024,512]{1,0:T(8,128)(2,1)}, u32[]{:S(2)}) copy-start(bf16[1024,512]{1,0:T(8,128)(2,1)} %param.10) | copy-start | bytes 3145732
  28.6 0.7 copy-start.6
  30.2 1.8 %copy-start.2 = (f32[16,16]{1,0:T(8,128)}, f32[16,16]{1,0:T(8,128)S(1)}, u32[]{:S(2)}) copy-start(f32[16,16]{1,0:T(8,128)S(1)} %get-tuple-element.11) | copy-start | bytes 3076
  32.0 0.7 copy-start.4
  32.6 10.5 %all-to-all-start.1 = ((f32[1,16,64]{2,0,1:T(1,128)}), f32[1,16,64]{2,0,1:T(1,128)}, u32[]{:S(2)}, u32[]{:S(2)}) async-start(f32[1,16,64]{2,0,1:T(1,128)} %bitcast.116), calls=%async_computation.1 | async-start | bytes 16384 | tf_op jit(solution)/shard_map/all_to_all | solution.py:52
  36.7 1.3 %copy-start.7 = (bf16[1,512]{1,0:T(2,128)(2,1)S(1)}, bf16[1,512]{1,0:T(2,128)(2,1)}, u32[]{:S(2)}) copy-start(bf16[1,512]{1,0:T(2,128)(2,1)} %param.9) | copy-start | bytes 3076
  38.1 0.7 copy-start.3
  39.2 1.3 %copy-start = (f32[16,16,1025]{2,1,0:T(8,128)S(1)}, f32[16,16,1025]{2,1,0:T(8,128)}, u32[]{:S(2)}) copy-start(f32[16,16,1025]{2,1,0:T(8,128)} %get-tuple-element.16) | copy-start | bytes 3148804
  39.2 1.3 %copy-start.5 = (f32[16,16]{1,0:T(8,128)S(1)}, f32[16,16]{1,0:T(8,128)}, u32[]{:S(2)}) copy-start(f32[16,16]{1,0:T(8,128)} %copy-done.4) | copy-start | bytes 3076
  43.2 11.7 %all-to-all-start.2 = ((f32[1,16,64]{2,0,1:T(1,128)}), f32[1,16,64]{2,0,1:T(1,128)S(1)}, u32[]{:S(2)}, u32[]{:S(2)}) async-start(f32[1,16,64]{2,0,1:T(1,128)} %bitcast.20), calls=%async_computation.2 | async-start | bytes 16384 | tf_op jit(solution)/shard_map/all_to_all | solution.py:53
  54.9 17.8 %all-to-all-start = ((f32[1,16,8192]{2,0,1:T(1,128)}), f32[1,16,8192]{2,0,1:T(1,128)S(1)}, u32[]{:S(2)}, u32[]{:S(2)}) async-start(f32[1,16,8192]{2,0,1:T(1,128)} %broadcast_in_dim.55), calls=%async_computation | async-start | bytes 1048576 | tf_op jit(solution)/shard_map/all_to_all | solution.py:51
where the time goes:
time: 75 us; the launch traced here: 74.4 us
  blocking collectives  24.9 us (33%)
  waiting for transfers between devices  17.6 us (23%)
  starting transfers between devices  13 us (17%)
  other arithmetic  7.23 us (10%)
  local copies, waits for them, and re-layouts  6.58 us (9%)
  matrix products  4.12 us (5%)
  between operations  0.93 us (1%)
    all_gather x1, blocking collectives, body(): gathered = lax.all_gather(queries, 'ctx', axis=0, tiled=True)  24.9 us
    all_to_all x1, waiting for transfers between devices, body(): lax.all_to_all(block_sum[None], 'ctx', split_axis=1, concat_axis=0, tiled...  12.1 us
    all_to_all x1, starting transfers between devices, body(): lax.all_to_all(block_total[None], 'ctx', split_axis=1, concat_axis=0, til...  5.35 us
    all_to_all x1, waiting for transfers between devices, body(): lax.all_to_all(block_total[None], 'ctx', split_axis=1, concat_axis=0, til...  4.99 us
    all_to_all x1, starting transfers between devices, body(): lax.all_to_all(block_max[None], 'ctx', split_axis=1, concat_axis=0, tiled...  4.08 us
    all_to_all x1, starting transfers between devices, body(): lax.all_to_all(block_sum[None], 'ctx', split_axis=1, concat_axis=0, tiled...  3.57 us
    unnamed x24, local copies, waits for them, and re-layouts  3.45 us
    dot_general x4, matrix products, body(): jnp.einsum('ngd,kd->ngk', query_part, key_part, preferred_element_type=jn...  2.63 us
  transfers between devices with their start and end apart: 3, of which 3 were waited for; matrix products, arithmetic and copies ran while one was open for 11% of the time, Pallas kernels for 0%

commit v1 on v0

--- a/solution.py
+++ b/solution.py
@@ -17,7 +17,21 @@
     query_heads = kv_heads * group_size
     all_keys = jnp.concatenate([cache_keys, fresh_keys], axis=0)
     all_values = jnp.concatenate([stored_values, fresh_values], axis=0)
-    gathered = lax.all_gather(queries, "ctx", axis=0, tiled=True)
+    ways, here, turn = (lax.axis_size("ctx"), lax.axis_index("ctx"), queries.shape[0])
+    shape = [n * ways if d == 0 else n for d, n in enumerate(queries.shape)]
+    full = lax.dynamic_update_slice_in_dim(
+        jnp.zeros(shape, queries.dtype), queries, here * turn, axis=0
+    )
+    going_up = going_down = queries
+    for far in range(1, ways // 2 + 1):
+        going_up = lax.ppermute(going_up, "ctx", [(d, (d + 1) % ways) for d in range(ways)])
+        full = lax.dynamic_update_slice_in_dim(full, going_up, (here - far) % ways * turn, axis=0)
+        if 2 * far < ways:
+            going_down = lax.ppermute(going_down, "ctx", [(d, (d - 1) % ways) for d in range(ways)])
+            full = lax.dynamic_update_slice_in_dim(
+                full, going_down, (here + far) % ways * turn, axis=0
+            )
+    gathered = full
     total_new = gathered.shape[0]
     key_order = lax.dynamic_slice_in_dim(positions, device_rank * new_rows, new_rows, 0)
     live = jnp.arange(cache_rows, dtype=jnp.int32) < cache_lengths[0]

time: 75 us -> 99 us (1.32)
  starting transfers between devices: 13 us -> 45 us
  blocking collectives: 24.9 us -> 0 us
  waiting for transfers between devices: 17.6 us -> 31.6 us
  local copies, waits for them, and re-layouts: 6.58 us -> 12.2 us
  other arithmetic: 7.23 us -> 5.14 us
    ppermute x0 -> x15, starting transfers between devices: none -> 32.2 us  [the longest x7 31.7 us: body(): lax.ppermute(going_down, 'ctx', [(d, (d - 1) % ways) for d in range(ways)])]
    all_gather x1 -> x0, blocking collectives: 24.9 us -> none  [body(): gathered = lax.all_gather(queries, 'ctx', axis=0, tiled=True)]
    dynamic_update_slice x0 -> x16, local copies, waits for them, and re-layouts: none -> 7.6 us  [the longest x8 3.8 us: body(): lax.dynamic_update_slice_in_dim(full, going_up, (here - far) % ways * tur...]
    ppermute x0 -> x15, waiting for transfers between devices: none -> 6.93 us  [the longest x7 6.39 us: body(): lax.ppermute(going_down, 'ctx', [(d, (d - 1) % ways) for d in range(ways)])]
    all_to_all x1, waiting for transfers between devices: 0.56 us -> 5.5 us  [body(): lax.all_to_all(block_max[None], 'ctx', split_axis=1, concat_axis=0, tiled...]
    all_to_all x1, waiting for transfers between devices: 12.1 us -> 14.2 us  [body(): lax.all_to_all(block_sum[None], 'ctx', split_axis=1, concat_axis=0, tiled...]
    unnamed x24 -> x19, local copies, waits for them, and re-layouts: 3.45 us -> 1.46 us
    all_to_all x1, starting transfers between devices: 5.35 us -> 3.41 us  [body(): lax.all_to_all(block_total[None], 'ctx', split_axis=1, concat_axis=0, til...]
  transfers between devices with their start and end apart: 3 -> 18, of which waited for: 3 -> 9; matrix products, arithmetic and copies ran while one was open for 11% -> 14% of each run, Pallas kernels for 0% -> 0%
where the time goes in v1:
time: 99 us; the launch traced here: 98.6 us
  starting transfers between devices  45 us (45%)
  waiting for transfers between devices  31.6 us (32%)
  local copies, waits for them, and re-layouts  12.2 us (12%)
  other arithmetic  5.14 us (5%)
  matrix products  3.19 us (3%)
  between operations  1.46 us (1%)
    ppermute x7, starting transfers between devices, body(): lax.ppermute(going_down, 'ctx', [(d, (d - 1) % ways) for d in range(ways)])  31.7 us
    all_to_all x1, waiting for transfers between devices, body(): lax.all_to_all(block_sum[None], 'ctx', split_axis=1, concat_axis=0, tiled...  14.2 us
    ppermute x7, waiting for transfers between devices, body(): lax.ppermute(going_down, 'ctx', [(d, (d - 1) % ways) for d in range(ways)])  6.39 us
    all_to_all x1, starting transfers between devices, body(): lax.all_to_all(block_max[None], 'ctx', split_axis=1, concat_axis=0, tiled...  5.81 us
    all_to_all x1, waiting for transfers between devices, body(): lax.all_to_all(block_max[None], 'ctx', split_axis=1, concat_axis=0, tiled...  5.5 us
    all_to_all x1, waiting for transfers between devices, body(): lax.all_to_all(block_total[None], 'ctx', split_axis=1, concat_axis=0, til...  5.01 us
    dynamic_update_slice x8, local copies, waits for them, and re-layouts, body(): lax.dynamic_update_slice_in_dim(full, going_up, (here - far) % ways * tur...  3.8 us
    all_to_all x1, starting transfers between devices, body(): lax.all_to_all(block_sum[None], 'ctx', split_axis=1, concat_axis=0, tiled...  3.57 us
  transfers between devices with their start and end apart: 18, of which 9 were waited for; matrix products, arithmetic and copies ran while one was open for 14% of the time, Pallas kernels for 0%

profile of v1, /device:TPU:0, one launch (start us, length us, event | category | flops | bytes accessed | tf_op | source)
XLA Modules:
  0.0 98.6 jit_solution(16312736999738076978)
XLA Ops:
  0.0 0.5 collective-permute-start
  0.5 5.0 %collective-permute-start.1 = (bf16[1,8192]{1,0:T(2,128)(2,1)}, bf16[1,8192]{1,0:T(2,128)(2,1)S(1)}, u32[]{:S(2)}, u32[]{:S(2)}) collective-permute-start(bf16[1,8192]{1,0:T(2,128)(2,1)} %param.7), channel_id=1, source_target_pairs={{0,15},{1,0},{2,1},{3,2},{4,3},{5,4},{6,5},{7,6},{8,7},{9,8},{10,9... | collective-permute-start | bytes 49160 | tf_op jit(solution)/shard_map/ppermute | solution.py:30
  5.5 1.2 %dynamic_slice.3 = s32[1]{0:T(128)} dynamic-slice(s32[16]{0:T(128)} %param.13, s32[]{:T(128)S(6)} %select_n.125), dynamic_slice_sizes={1} | dynamic-slice | bytes 12 | tf_op jit(solution)/shard_map/dynamic_slice | solution.py:36
  6.7 0.5 collective-permute-done
  7.3 1.3 %compare_bitcast_fusion = pred[16,1]{0,1:T(4,128)(4,1)S(1)} fusion(s32[16]{0:T(128)} %param.13, s32[]{:T(128)} %bitcast.1), kind=kLoop, calls=%fused_computation.52 | loop fusion | flops 16 | bytes 84 | tf_op jit(solution)/shard_map/le | solution.py:39
  9.2 4.5 %collective-permute-start.3 = (bf16[1,8192]{1,0:T(2,128)(2,1)S(1)}, bf16[1,8192]{1,0:T(2,128)(2,1)S(1)}, u32[]{:S(2)}, u32[]{:S(2)}) collective-permute-start(bf16[1,8192]{1,0:T(2,128)(2,1)S(1)} %collective-permute-done.1), channel_id=1, source_target_pairs={{0,15},{1,0},{2,1},{3,2},{4,3},{5,4},{6,5},{7,6},{8,7},{9,8},{10,9... | collective-permute-start | bytes 49160 | tf_op jit(solution)/shard_map/ppermute | solution.py:30
  13.8 1.5 %collective-permute-done.3 = bf16[1,8192]{1,0:T(2,128)(2,1)S(1)} collective-permute-done((bf16[1,8192]{1,0:T(2,128)(2,1)S(1)}, bf16[1,8192]{1,0:T(2,128)(2,1)S(1)}, u32[]{:S(2)}, u32[]{:S(2)}) %collective-permute-start.3) | collective-permute-done | bytes 16416 | tf_op jit(solution)/shard_map/ppermute | solution.py:30
  15.3 4.5 %collective-permute-start.5 = (bf16[1,8192]{1,0:T(2,128)(2,1)S(1)}, bf16[1,8192]{1,0:T(2,128)(2,1)S(1)}, u32[]{:S(2)}, u32[]{:S(2)}) collective-permute-start(bf16[1,8192]{1,0:T(2,128)(2,1)S(1)} %collective-permute-done.3), channel_id=1, source_target_pairs={{0,15},{1,0},{2,1},{3,2},{4,3},{5,4},{6,5},{7,6},{8,7},{9,8},{10,9... | collective-permute-start | bytes 49160 | tf_op jit(solution)/shard_map/ppermute | solution.py:30
  19.8 1.6 %collective-permute-done.5 = bf16[1,8192]{1,0:T(2,128)(2,1)S(1)} collective-permute-done((bf16[1,8192]{1,0:T(2,128)(2,1)S(1)}, bf16[1,8192]{1,0:T(2,128)(2,1)S(1)}, u32[]{:S(2)}, u32[]{:S(2)}) %collective-permute-start.5) | collective-permute-done | bytes 16416 | tf_op jit(solution)/shard_map/ppermute | solution.py:30
  21.4 4.4 %collective-permute-start.7 = (bf16[1,8192]{1,0:T(2,128)(2,1)S(1)}, bf16[1,8192]{1,0:T(2,128)(2,1)S(1)}, u32[]{:S(2)}, u32[]{:S(2)}) collective-permute-start(bf16[1,8192]{1,0:T(2,128)(2,1)S(1)} %collective-permute-done.5), channel_id=1, source_target_pairs={{0,15},{1,0},{2,1},{3,2},{4,3},{5,4},{6,5},{7,6},{8,7},{9,8},{10,9... | collective-permute-start | bytes 49160 | tf_op jit(solution)/shard_map/ppermute | solution.py:30
  25.8 1.3 %constant_dynamic-update-slice_fusion.1 = bf16[1025,512]{1,0:T(8,128)(2,1)S(1)} fusion(bf16[1024,512]{1,0:T(8,128)(2,1)} %param.10), kind=kLoop, calls=%fused_computation.41 | loop fusion | bytes 2097152
  27.4 4.4 %collective-permute-start.9 = (bf16[1,8192]{1,0:T(2,128)(2,1)S(1)}, bf16[1,8192]{1,0:T(2,128)(2,1)S(1)}, u32[]{:S(2)}, u32[]{:S(2)}) collective-permute-start(bf16[1,8192]{1,0:T(2,128)(2,1)S(1)} %collective-permute-done.7), channel_id=1, source_target_pairs={{0,15},{1,0},{2,1},{3,2},{4,3},{5,4},{6,5},{7,6},{8,7},{9,8},{10,9... | collective-permute-start | bytes 49160 | tf_op jit(solution)/shard_map/ppermute | solution.py:30
  31.9 1.5 %collective-permute-done.9 = bf16[1,8192]{1,0:T(2,128)(2,1)S(1)} collective-permute-done((bf16[1,8192]{1,0:T(2,128)(2,1)S(1)}, bf16[1,8192]{1,0:T(2,128)(2,1)S(1)}, u32[]{:S(2)}, u32[]{:S(2)}) %collective-permute-start.9) | collective-permute-done | bytes 16416 | tf_op jit(solution)/shard_map/ppermute | solution.py:30
  33.5 4.4 %collective-permute-start.11 = (bf16[1,8192]{1,0:T(2,128)(2,1)S(1)}, bf16[1,8192]{1,0:T(2,128)(2,1)S(1)}, u32[]{:S(2)}, u32[]{:S(2)}) collective-permute-start(bf16[1,8192]{1,0:T(2,128)(2,1)S(1)} %collective-permute-done.9), channel_id=1, source_target_pairs={{0,15},{1,0},{2,1},{3,2},{4,3},{5,4},{6,5},{7,6},{8,7},{9,8},{10,9... | collective-permute-start | bytes 49160 | tf_op jit(solution)/shard_map/ppermute | solution.py:30
  37.9 1.6 %collective-permute-done.11 = bf16[1,8192]{1,0:T(2,128)(2,1)S(1)} collective-permute-done((bf16[1,8192]{1,0:T(2,128)(2,1)S(1)}, bf16[1,8192]{1,0:T(2,128)(2,1)S(1)}, u32[]{:S(2)}, u32[]{:S(2)}) %collective-permute-start.11) | collective-permute-done | bytes 16416 | tf_op jit(solution)/shard_map/ppermute | solution.py:30
  39.5 4.4 %collective-permute-start.13 = (bf16[1,8192]{1,0:T(2,128)(2,1)S(1)}, bf16[1,8192]{1,0:T(2,128)(2,1)S(1)}, u32[]{:S(2)}, u32[]{:S(2)}) collective-permute-start(bf16[1,8192]{1,0:T(2,128)(2,1)S(1)} %collective-permute-done.11), channel_id=1, source_target_pairs={{0,15},{1,0},{2,1},{3,2},{4,3},{5,4},{6,5},{7,6},{8,7},{9,8},{10,9... | collective-permute-start | bytes 49160 | tf_op jit(solution)/shard_map/ppermute | solution.py:30
  44.3 0.5 dynamic_update_slice.48
  44.9 0.5 dynamic_update_slice.49
  45.3 0.5 dynamic_update_slice.50
  45.8 0.5 dynamic_update_slice.51
  46.3 0.5 dynamic_update_slice.52
  46.8 0.5 dynamic_update_slice.53
  47.3 0.5 dynamic_update_slice.54
  47.8 0.5 dynamic_update_slice.55
  48.2 0.5 dynamic_update_slice.56
  48.7 0.5 dynamic_update_slice.57
  49.2 0.5 dynamic_update_slice.58
  49.7 0.5 dynamic_update_slice.59
  50.2 0.5 dynamic_update_slice.60
  50.7 0.5 dynamic_update_slice.61
  51.2 0.5 dynamic_update_slice.62
  51.7 0.5 dynamic_update_slice.63
  52.2 0.4 fusion.11
  52.6 0.4 fusion.12
  53.4 0.5 convert_reduce_fusion
  54.3 0.4 fusion.13
  55.2 0.7 pad_maximum_fusion.1
  56.3 0.5 convert_reduce_fusion.2
  57.1 5.8 %all-to-all-start.1 = ((f32[1,16,64]{2,0,1:T(1,128)}), f32[1,16,64]{2,0,1:T(1,128)S(1)}, u32[]{:S(2)}, u32[]{:S(2)}) async-start(f32[1,16,64]{2,0,1:T(1,128)} %bitcast.11), calls=%async_computation.1 | async-start | bytes 16384 | tf_op jit(solution)/shard_map/all_to_all | solution.py:66
  63.1 0.7 pad_maximum_fusion.2
  63.8 5.5 %all-to-all-done.1 = f32[1,16,64]{2,0,1:T(1,128)S(1)} async-done(((f32[1,16,64]{2,0,1:T(1,128)}), f32[1,16,64]{2,0,1:T(1,128)S(1)}, u32[]{:S(2)}, u32[]{:S(2)}) %all-to-all-start.1) | async-done | bytes 4128 | tf_op jit(solution)/shard_map/all_to_all | solution.py:66
  69.3 3.4 %all-to-all-start.2 = ((f32[1,16,64]{2,0,1:T(1,128)}), f32[1,16,64]{2,0,1:T(1,128)S(1)}, u32[]{:S(2)}, u32[]{:S(2)}) async-start(f32[1,16,64]{2,0,1:T(1,128)} %bitcast.15), calls=%async_computation.2 | async-start | bytes 16384 | tf_op jit(solution)/shard_map/all_to_all | solution.py:67
  72.8 1.3 %broadcast_in_dim.59 = f32[1,16,8192]{2,0,1:T(1,128)} reshape(f32[16,8192]{1,0:T(8,128)S(1)} %pad_maximum_fusion) | data formatting | bytes 1048576 | tf_op jit(solution)/shard_map/broadcast_in_dim | solution.py:65
  74.1 5.0 %all-to-all-done.2 = f32[1,16,64]{2,0,1:T(1,128)S(1)} async-done(((f32[1,16,64]{2,0,1:T(1,128)}), f32[1,16,64]{2,0,1:T(1,128)S(1)}, u32[]{:S(2)}, u32[]{:S(2)}) %all-to-all-start.2) | async-done | bytes 4128 | tf_op jit(solution)/shard_map/all_to_all | solution.py:67
  79.1 3.6 %all-to-all-start = ((f32[1,16,8192]{2,0,1:T(1,128)}), f32[1,16,8192]{2,0,1:T(1,128)S(1)}, u32[]{:S(2)}, u32[]{:S(2)}) async-start(f32[1,16,8192]{2,0,1:T(1,128)} %broadcast_in_dim.59), calls=%async_computation | async-start | bytes 1048576 | tf_op jit(solution)/shard_map/all_to_all | solution.py:65
  82.8 14.2 %all-to-all-done = f32[1,16,8192]{2,0,1:T(1,128)S(1)} async-done(((f32[1,16,8192]{2,0,1:T(1,128)}), f32[1,16,8192]{2,0,1:T(1,128)S(1)}, u32[]{:S(2)}, u32[]{:S(2)}) %all-to-all-start) | async-done | bytes 524320 | tf_op jit(solution)/shard_map/all_to_all | solution.py:65
  97.1 0.8 multiply_reduce_fusion
  98.0 0.7 divide_convert_fusion
  (55 shorter events, 3.1 us)
Async XLA Ops:
  0.0 31.9 %copy-start = (bf16[1024,512]{1,0:T(8,128)(2,1)S(1)}, bf16[1024,512]{1,0:T(8,128)(2,1)}, u32[]{:S(2)}) copy-start(bf16[1024,512]{1,0:T(8,128)(2,1)} %param.11) | copy-start | bytes 3145732
  0.0 7.3 %collective-permute-start = (bf16[1,8192]{1,0:T(2,128)(2,1)}, bf16[1,8192]{1,0:T(2,128)(2,1)S(1)}, u32[]{:S(2)}, u32[]{:S(2)}) collective-permute-start(bf16[1,8192]{1,0:T(2,128)(2,1)} %param.7), channel_id=1, source_target_pairs={{0,1},{1,2},{2,3},{3,4},{4,5},{5,6},{6,7},{7,8},{8,9},{9,10},{10,1... | collective-permute-start | bytes 49160 | tf_op jit(solution)/shard_map/ppermute | solution.py:27
  0.5 8.7 %collective-permute-start.1 = (bf16[1,8192]{1,0:T(2,128)(2,1)}, bf16[1,8192]{1,0:T(2,128)(2,1)S(1)}, u32[]{:S(2)}, u32[]{:S(2)}) collective-permute-start(bf16[1,8192]{1,0:T(2,128)(2,1)} %param.7), channel_id=1, source_target_pairs={{0,15},{1,0},{2,1},{3,2},{4,3},{5,4},{6,5},{7,6},{8,7},{9,8},{10,9... | collective-permute-start | bytes 49160 | tf_op jit(solution)/shard_map/ppermute | solution.py:30
  7.3 6.5 %collective-permute-start.2 = (bf16[1,8192]{1,0:T(2,128)(2,1)S(1)}, bf16[1,8192]{1,0:T(2,128)(2,1)S(1)}, u32[]{:S(2)}, u32[]{:S(2)}) collective-permute-start(bf16[1,8192]{1,0:T(2,128)(2,1)S(1)} %collective-permute-done), channel_id=1, source_target_pairs={{0,1},{1,2},{2,3},{3,4},{4,5},{5,6},{6,7},{7,8},{8,9},{9,10},{10,1... | collective-permute-start | bytes 49160 | tf_op jit(solution)/shard_map/ppermute | solution.py:27
  9.2 6.1 %collective-permute-start.3 = (bf16[1,8192]{1,0:T(2,128)(2,1)S(1)}, bf16[1,8192]{1,0:T(2,128)(2,1)S(1)}, u32[]{:S(2)}, u32[]{:S(2)}) collective-permute-start(bf16[1,8192]{1,0:T(2,128)(2,1)S(1)} %collective-permute-done.1), channel_id=1, source_target_pairs={{0,15},{1,0},{2,1},{3,2},{4,3},{5,4},{6,5},{7,6},{8,7},{9,8},{10,9... | collective-permute-start | bytes 49160 | tf_op jit(solution)/shard_map/ppermute | solution.py:30
  13.7 6.1 %collective-permute-start.4 = (bf16[1,8192]{1,0:T(2,128)(2,1)S(1)}, bf16[1,8192]{1,0:T(2,128)(2,1)S(1)}, u32[]{:S(2)}, u32[]{:S(2)}) collective-permute-start(bf16[1,8192]{1,0:T(2,128)(2,1)S(1)} %collective-permute-done.2), channel_id=1, source_target_pairs={{0,1},{1,2},{2,3},{3,4},{4,5},{5,6},{6,7},{7,8},{8,9},{9,10},{10,1... | collective-permute-start | bytes 49160 | tf_op jit(solution)/shard_map/ppermute | solution.py:27
  15.3 6.1 %collective-permute-start.5 = (bf16[1,8192]{1,0:T(2,128)(2,1)S(1)}, bf16[1,8192]{1,0:T(2,128)(2,1)S(1)}, u32[]{:S(2)}, u32[]{:S(2)}) collective-permute-start(bf16[1,8192]{1,0:T(2,128)(2,1)S(1)} %collective-permute-done.3), channel_id=1, source_target_pairs={{0,15},{1,0},{2,1},{3,2},{4,3},{5,4},{6,5},{7,6},{8,7},{9,8},{10,9... | collective-permute-start | bytes 49160 | tf_op jit(solution)/shard_map/ppermute | solution.py:30
  19.8 6.0 %collective-permute-start.6 = (bf16[1,8192]{1,0:T(2,128)(2,1)S(1)}, bf16[1,8192]{1,0:T(2,128)(2,1)S(1)}, u32[]{:S(2)}, u32[]{:S(2)}) collective-permute-start(bf16[1,8192]{1,0:T(2,128)(2,1)S(1)} %collective-permute-done.4), channel_id=1, source_target_pairs={{0,1},{1,2},{2,3},{3,4},{4,5},{5,6},{6,7},{7,8},{8,9},{9,10},{10,1... | collective-permute-start | bytes 49160 | tf_op jit(solution)/shard_map/ppermute | solution.py:27
  21.4 6.0 %collective-permute-start.7 = (bf16[1,8192]{1,0:T(2,128)(2,1)S(1)}, bf16[1,8192]{1,0:T(2,128)(2,1)S(1)}, u32[]{:S(2)}, u32[]{:S(2)}) collective-permute-start(bf16[1,8192]{1,0:T(2,128)(2,1)S(1)} %collective-permute-done.5), channel_id=1, source_target_pairs={{0,15},{1,0},{2,1},{3,2},{4,3},{5,4},{6,5},{7,6},{8,7},{9,8},{10,9... | collective-permute-start | bytes 49160 | tf_op jit(solution)/shard_map/ppermute | solution.py:30
  25.8 6.0 %collective-permute-start.8 = (bf16[1,8192]{1,0:T(2,128)(2,1)S(1)}, bf16[1,8192]{1,0:T(2,128)(2,1)S(1)}, u32[]{:S(2)}, u32[]{:S(2)}) collective-permute-start(bf16[1,8192]{1,0:T(2,128)(2,1)S(1)} %collective-permute-done.6), channel_id=1, source_target_pairs={{0,1},{1,2},{2,3},{3,4},{4,5},{5,6},{6,7},{7,8},{8,9},{9,10},{10,1... | collective-permute-start | bytes 49160 | tf_op jit(solution)/shard_map/ppermute | solution.py:27
  27.1 10.8 %copy-start.4 = (bf16[1,512]{1,0:T(2,128)(2,1)S(1)}, bf16[1,512]{1,0:T(2,128)(2,1)}, u32[]{:S(2)}) copy-start(bf16[1,512]{1,0:T(2,128)(2,1)} %param.8) | copy-start | bytes 3076
  27.1 16.8 %copy-start.5 = (bf16[1,512]{1,0:T(2,128)(2,1)S(1)}, bf16[1,512]{1,0:T(2,128)(2,1)}, u32[]{:S(2)}) copy-start(bf16[1,512]{1,0:T(2,128)(2,1)} %param.9) | copy-start | bytes 3076
  27.2 17.1 %copy-start.1 = (bf16[1,8192]{1,0:T(2,128)(2,1)S(1)}, bf16[1,8192]{1,0:T(2,128)(2,1)}, u32[]{:S(2)}) copy-start(bf16[1,8192]{1,0:T(2,128)(2,1)} %param.7) | copy-start | bytes 49156
  27.4 6.0 %collective-permute-start.9 = (bf16[1,8192]{1,0:T(2,128)(2,1)S(1)}, bf16[1,8192]{1,0:T(2,128)(2,1)S(1)}, u32[]{:S(2)}, u32[]{:S(2)}) collective-permute-start(bf16[1,8192]{1,0:T(2,128)(2,1)S(1)} %collective-permute-done.7), channel_id=1, source_target_pairs={{0,15},{1,0},{2,1},{3,2},{4,3},{5,4},{6,5},{7,6},{8,7},{9,8},{10,9... | collective-permute-start | bytes 49160 | tf_op jit(solution)/shard_map/ppermute | solution.py:30
  31.9 6.0 %collective-permute-start.10 = (bf16[1,8192]{1,0:T(2,128)(2,1)S(1)}, bf16[1,8192]{1,0:T(2,128)(2,1)S(1)}, u32[]{:S(2)}, u32[]{:S(2)}) collective-permute-start(bf16[1,8192]{1,0:T(2,128)(2,1)S(1)} %collective-permute-done.8), channel_id=1, source_target_pairs={{0,1},{1,2},{2,3},{3,4},{4,5},{5,6},{6,7},{7,8},{8,9},{9,10},{10,1... | collective-permute-start | bytes 49160 | tf_op jit(solution)/shard_map/ppermute | solution.py:27
  33.5 6.0 %collective-permute-start.11 = (bf16[1,8192]{1,0:T(2,128)(2,1)S(1)}, bf16[1,8192]{1,0:T(2,128)(2,1)S(1)}, u32[]{:S(2)}, u32[]{:S(2)}) collective-permute-start(bf16[1,8192]{1,0:T(2,128)(2,1)S(1)} %collective-permute-done.9), channel_id=1, source_target_pairs={{0,15},{1,0},{2,1},{3,2},{4,3},{5,4},{6,5},{7,6},{8,7},{9,8},{10,9... | collective-permute-start | bytes 49160 | tf_op jit(solution)/shard_map/ppermute | solution.py:30
  37.9 6.0 %copy-start.2 = (bf16[1,8192]{1,0:T(2,128)(2,1)}, bf16[1,8192]{1,0:T(2,128)(2,1)S(1)}, u32[]{:S(2)}) copy-start(bf16[1,8192]{1,0:T(2,128)(2,1)S(1)} %collective-permute-done.10) | copy-start | bytes 49156
  37.9 6.0 %collective-permute-start.12 = (bf16[1,8192]{1,0:T(2,128)(2,1)S(1)}, bf16[1,8192]{1,0:T(2,128)(2,1)S(1)}, u32[]{:S(2)}, u32[]{:S(2)}) collective-permute-start(bf16[1,8192]{1,0:T(2,128)(2,1)S(1)} %collective-permute-done.10), channel_id=1, source_target_pairs={{0,1},{1,2},{2,3},{3,4},{4,5},{5,6},{6,7},{7,8},{8,9},{9,10},{10,1... | collective-permute-start | bytes 49160 | tf_op jit(solution)/shard_map/ppermute | solution.py:27
  39.5 11.7 %collective-permute-start.13 = (bf16[1,8192]{1,0:T(2,128)(2,1)S(1)}, bf16[1,8192]{1,0:T(2,128)(2,1)S(1)}, u32[]{:S(2)}, u32[]{:S(2)}) collective-permute-start(bf16[1,8192]{1,0:T(2,128)(2,1)S(1)} %collective-permute-done.11), channel_id=1, source_target_pairs={{0,15},{1,0},{2,1},{3,2},{4,3},{5,4},{6,5},{7,6},{8,7},{9,8},{10,9... | collective-permute-start | bytes 49160 | tf_op jit(solution)/shard_map/ppermute | solution.py:30
  43.9 7.7 %collective-permute-start.14 = (bf16[1,8192]{1,0:T(2,128)(2,1)S(1)}, bf16[1,8192]{1,0:T(2,128)(2,1)S(1)}, u32[]{:S(2)}, u32[]{:S(2)}) collective-permute-start(bf16[1,8192]{1,0:T(2,128)(2,1)S(1)} %collective-permute-done.12), channel_id=1, source_target_pairs={{0,1},{1,2},{2,3},{3,4},{4,5},{5,6},{6,7},{7,8},{8,9},{9,10},{10,1... | collective-permute-start | bytes 49160 | tf_op jit(solution)/shard_map/ppermute | solution.py:27
  44.0 5.7 %copy-start.3 = (bf16[1,8192]{1,0:T(2,128)(2,1)S(1)}, bf16[1,8192]{1,0:T(2,128)(2,1)}, u32[]{:S(2)}) copy-start(bf16[1,8192]{1,0:T(2,128)(2,1)} %copy-done.2) | copy-start | bytes 49156
  57.1 12.2 %all-to-all-start.1 = ((f32[1,16,64]{2,0,1:T(1,128)}), f32[1,16,64]{2,0,1:T(1,128)S(1)}, u32[]{:S(2)}, u32[]{:S(2)}) async-start(f32[1,16,64]{2,0,1:T(1,128)} %bitcast.11), calls=%async_computation.1 | async-start | bytes 16384 | tf_op jit(solution)/shard_map/all_to_all | solution.py:66
  69.3 9.8 %all-to-all-start.2 = ((f32[1,16,64]{2,0,1:T(1,128)}), f32[1,16,64]{2,0,1:T(1,128)S(1)}, u32[]{:S(2)}, u32[]{:S(2)}) async-start(f32[1,16,64]{2,0,1:T(1,128)} %bitcast.15), calls=%async_computation.2 | async-start | bytes 16384 | tf_op jit(solution)/shard_map/all_to_all | solution.py:67
  79.1 17.8 %all-to-all-start = ((f32[1,16,8192]{2,0,1:T(1,128)}), f32[1,16,8192]{2,0,1:T(1,128)S(1)}, u32[]{:S(2)}, u32[]{:S(2)}) async-start(f32[1,16,8192]{2,0,1:T(1,128)} %broadcast_in_dim.59), calls=%async_computation | async-start | bytes 1048576 | tf_op jit(solution)/shard_map/all_to_all | solution.py:65
